TPU v7x, 32 devices: a whole 2x2x4 slice. The times are simulated.
32 devices in a mesh: seq: 16 (over z, y, x), wa: 2 (over core).
Axes of the slice: x: 2, y: 2, z: 4, core: 2. Of those that a mesh axis runs over, the one named last changes fastest.
Arguments:
- tokens: bfloat16 [2, 5120, 768], P('wa', 'seq'), may hold values from -6 to 6
- cotangent: bfloat16 [2, 5120, 768], P('wa', 'seq'), may hold values from -6 to 6
- w_qkv: bfloat16 [3, 768, 768], P(None, None, 'wa'), may hold values from -0.21875 to 0.21875
- w_out: bfloat16 [768, 768], P('wa'), may hold values from -0.875 to 0.875
- w_up: bfloat16 [768, 3072], P(None, 'wa'), may hold values from -0.21875 to 0.21875
- w_down: bfloat16 [3072, 768], P('wa'), may hold values from -0.109375 to 0.109375
- gain_attn: bfloat16 [768], P('wa'), may hold values from 0.25 to 1.75
- gain_mlp: bfloat16 [768], P('wa'), may hold values from 0.25 to 1.75
- router: bfloat16 [768], P('wa'), may hold values from -0.21875 to 0.21875
- picked: int32 [2, 1280], replicated, may hold values from 0 to 319, as said below
- counts: int32 [2, 16], replicated, may hold values from 1 to 80, as said below
Outputs:
- mixed: bfloat16 [2, 5120, 768], P('wa', 'seq')
- grad_tokens: bfloat16 [2, 5120, 768], P('wa', 'seq')
- grad_qkv: float32 [3, 768, 768], P(None, None, 'wa')
- grad_out: float32 [768, 768], P('wa')
- grad_up: float32 [768, 3072], P(None, 'wa')
- grad_down: float32 [3072, 768], P('wa')
- grad_gain_attn: float32 [768], P('wa')
- grad_gain_mlp: float32 [768], P('wa')
- grad_router: float32 [768], P('wa')
Inputs may be any that keep to these rules, and one draw needn't show every extreme that they name: For stream s and device d, entries d * 80 to d * 80 + counts[s, d] - 1 of picked[s] are the indices of that device's selected tokens within its block; the 80 entries of one device are distinct. `counts`: selected tokens of stream s on device d; in each stream some device has exactly 80.
All inputs are finite; a program needn't handle non-finite values.
Results may differ from a plain program's by a relative error of at most 0.014.
The roundings to bfloat16 on the way count: a program that leaves them out, or rounds other values in their place, can miss the bound.
Values may be sent and summed in bfloat16 or wider, within the bound.
A program may use at most 320 MiB of HBM per device.

v0:
```python
import jax
import jax.numpy as jnp
from jax import lax
from jax.sharding import PartitionSpec as P

HD = 64
CAP = 80
EPS = 1e-05
NEG = -1e30


def norm_rows(value, gain):
    scale = lax.rsqrt(jnp.mean(value * value, axis=-1, keepdims=True) + EPS)
    return (value * scale * gain, scale)


def norm_back(value, scale, gain, grad_out):
    normed = value * scale
    weighted = grad_out * gain
    grad_value = scale * (weighted - normed * jnp.mean(weighted * normed, axis=-1, keepdims=True))
    return (grad_value, normed)


def gelu_back(pre, grad):
    unused, pull = jax.vjp(lambda value: jax.nn.gelu(value, approximate=True), pre)
    return pull(grad)[0]


def body(
    tokens, cotangent, w_qkv, w_out, w_up, w_down, gain_attn, gain_mlp, router, picked, counts
):
    f32 = jnp.float32
    bf16 = jnp.bfloat16
    nseq = lax.axis_size("seq")
    me = lax.axis_index("seq")
    side = lax.axis_index("wa")
    slots = jnp.arange(CAP, dtype=jnp.int32)
    own_rows = lax.dynamic_slice(picked, (side, me * CAP), (1, CAP))[0]
    x_own = jnp.take(tokens[0], own_rows, axis=0)
    dy_own = jnp.take(cotangent[0], own_rows, axis=0).astype(f32)
    x_rows, g_attn, g_mlp, w_router = (
        lax.all_gather(x_own[None], "wa", axis=0, tiled=True),
        lax.all_gather(gain_attn, "wa", axis=0, tiled=True),
        lax.all_gather(gain_mlp, "wa", axis=0, tiled=True),
        lax.all_gather(router, "wa", axis=0, tiled=True),
    )
    qkv_w, out_w, up_w, down_w = (w_qkv, w_out, w_up, w_down)
    streams = jnp.arange(lax.axis_size("wa"))
    stream_picked = jnp.take(picked, streams, axis=0)
    stream_counts = jnp.take(counts, streams, axis=0)
    key_index = jnp.arange(nseq * CAP, dtype=jnp.int32)
    key_device = key_index // CAP
    key_pos = stream_picked * nseq + key_device[None, :]
    key_live = (key_index % CAP)[None, :] < jnp.take(stream_counts, key_device, axis=1)
    query_index = me * CAP + slots
    query_pos = lax.dynamic_slice_in_dim(key_pos, me * CAP, CAP, 1)
    own_live = (slots < counts[side, me]).astype(f32)
    gains_a = g_attn.astype(f32)
    gains_m = g_mlp.astype(f32)
    x_keep = x_own.astype(f32)
    weight = jax.nn.sigmoid(jnp.dot(x_own, w_router, preferred_element_type=f32))
    x_wide = x_rows.astype(f32)
    normed_a, scale_a = norm_rows(x_wide, gains_a)
    u_rows = normed_a.astype(bf16)
    qkv = jnp.einsum("srd,cde->csre", u_rows, qkv_w, preferred_element_type=f32).astype(bf16)
    query = qkv[0]
    local_kv = qkv[1:]
    batch = query.shape[0]
    heads = query.shape[-1] // HD
    factor = HD ** (-0.5)
    split_q = query.reshape(batch, CAP, heads, HD)
    kv_all = lax.all_gather(local_kv, "seq", axis=2, tiled=True)
    block = 8 * CAP
    nblock = kv_all.shape[2] // block

    def block_of(start):
        keys_b = lax.dynamic_slice_in_dim(kv_all[0], start, block, 1).reshape(
            batch, block, heads, HD
        )
        vals_b = lax.dynamic_slice_in_dim(kv_all[1], start, block, 1).reshape(
            batch, block, heads, HD
        )
        k_pos = lax.dynamic_slice_in_dim(key_pos, start, block, 1)
        k_live = lax.dynamic_slice_in_dim(key_live, start, block, 1)
        k_index = start + jnp.arange(block, dtype=jnp.int32)
        allowed = (k_pos[:, None, :] <= query_pos[:, :, None]) & (
            k_live[:, None, :] | (k_index[None, None, :] == query_index[None, :, None])
        )
        raw = jnp.einsum("sqhd,skhd->shqk", split_q, keys_b, preferred_element_type=f32) * factor
        return (keys_b, vals_b, allowed, jnp.where(allowed[:, None], raw, NEG))

    def max_sum(number, carry):
        top, total = carry
        unused_k, unused_v, allowed, scores = block_of(number * block)
        new_top = jnp.maximum(top, jnp.max(scores, axis=-1, keepdims=True))
        expd = jnp.where(allowed[:, None], jnp.exp(scores - new_top), 0.0)
        return (new_top, total * jnp.exp(top - new_top) + jnp.sum(expd, axis=-1, keepdims=True))

    top_start = jnp.full((batch, heads, CAP, 1), NEG, f32)
    top, total = lax.fori_loop(
        0, nblock, max_sum, (top_start, jnp.zeros((batch, heads, CAP, 1), f32))
    )
    lse = top + jnp.log(total)

    def weigh(number, acc):
        unused_k, vals_b, allowed, scores = block_of(number * block)
        probs_low = jnp.exp(scores - lse).astype(bf16)
        return acc + jnp.einsum("shqk,skhd->sqhd", probs_low, vals_b, preferred_element_type=f32)

    acc = lax.fori_loop(0, nblock, weigh, jnp.zeros((batch, CAP, heads, HD), f32))
    attended = acc.reshape(query.shape).astype(bf16)
    attn_part = jnp.einsum("sqe,ed->sqd", attended, out_w, preferred_element_type=f32)
    attn_own = lax.psum_scatter(attn_part, "wa", scatter_dimension=0, tiled=True)[0]
    resid = x_keep + attn_own
    normed_m, scale_m = norm_rows(resid, gains_m)
    w_own = normed_m.astype(bf16)
    w_rows = lax.all_gather(w_own[None], "wa", axis=0, tiled=True)
    pre = jnp.einsum("srd,df->srf", w_rows, up_w, preferred_element_type=f32)
    act = jax.nn.gelu(pre, approximate=True).astype(bf16)
    mlp_part = jnp.einsum("srf,fd->srd", act, down_w, preferred_element_type=f32)
    mlp_own = lax.psum_scatter(
        mlp_part.astype(jnp.bfloat16), "wa", scatter_dimension=0, tiled=True
    ).astype(jnp.float32)[0]
    branch = attn_own + mlp_own
    lift = (weight * own_live)[:, None]
    out_rows = (x_keep + lift * branch).astype(bf16)
    mixed_out = tokens.at[0, own_rows].set(out_rows)
    grad_branch = dy_own * lift
    grad_logit = jnp.sum(dy_own * branch, axis=-1) * own_live * weight * (1.0 - weight)
    grad_router = jnp.dot(grad_logit, x_keep, precision=lax.Precision.HIGHEST)
    grad_m = grad_branch.astype(bf16)
    grad_m_rows = lax.all_gather(grad_m[None], "wa", axis=0, tiled=True)
    grad_down = jnp.einsum("srf,srd->fd", act, grad_m_rows, preferred_element_type=f32)
    grad_act = jnp.einsum("srd,fd->srf", grad_m_rows, down_w, preferred_element_type=f32)
    grad_pre = gelu_back(pre, grad_act).astype(bf16)
    grad_up = jnp.einsum("srd,srf->df", w_rows, grad_pre, preferred_element_type=f32)
    grad_w_part = jnp.einsum("srf,df->srd", grad_pre, up_w, preferred_element_type=f32)
    grad_w_own = lax.psum_scatter(grad_w_part, "wa", scatter_dimension=0, tiled=True)[0]
    grad_resid, hat_m = norm_back(resid, scale_m, gains_m, grad_w_own)
    grad_gain_m = jnp.sum(grad_w_own * hat_m, axis=0)
    grad_a = (grad_branch + grad_resid).astype(bf16)
    grad_a_rows = lax.all_gather(grad_a[None], "wa", axis=0, tiled=True)
    grad_out = jnp.einsum("sqe,sqd->ed", attended, grad_a_rows, preferred_element_type=f32)
    grad_attended = jnp.einsum(
        "sqd,ed->sqe", grad_a_rows, out_w, preferred_element_type=f32
    ).astype(bf16)
    split_do = grad_attended.reshape(batch, CAP, heads, HD)

    def delta_step(number, delta):
        unused_k, vals_b, allowed, scores = block_of(number * block)
        probs = jnp.exp(scores - lse)
        grad_probs = jnp.einsum("sqhd,skhd->shqk", split_do, vals_b, preferred_element_type=f32)
        return delta + jnp.sum(grad_probs * probs, axis=-1, keepdims=True)

    delta = lax.fori_loop(0, nblock, delta_step, jnp.zeros((batch, heads, CAP, 1), f32))

    def grad_step(number, carry):
        grad_query, holder = carry
        start = number * block
        keys_b, vals_b, allowed, scores = block_of(start)
        probs = jnp.exp(scores - lse)
        grad_probs = jnp.einsum("sqhd,skhd->shqk", split_do, vals_b, preferred_element_type=f32)
        grad_scores = (probs * (grad_probs - delta)).astype(bf16)
        grad_query = (
            grad_query
            + jnp.einsum("shqk,skhd->sqhd", grad_scores, keys_b, preferred_element_type=f32)
            * factor
        )
        grad_keys = (
            jnp.einsum("shqk,sqhd->skhd", grad_scores, split_q, preferred_element_type=f32) * factor
        )
        grad_values = jnp.einsum(
            "shqk,sqhd->skhd", probs.astype(bf16), split_do, preferred_element_type=f32
        )
        paired = jnp.stack([grad_keys, grad_values]).reshape(2, batch, block, heads * HD)
        holder = lax.dynamic_update_slice_in_dim(holder, paired, start, 2)
        return (grad_query, holder)

    grad_query, holder = lax.fori_loop(
        0,
        nblock,
        grad_step,
        (jnp.zeros((batch, CAP, heads, HD), f32), jnp.zeros(kv_all.shape, f32)),
    )
    kv_total = lax.psum_scatter(holder.astype(bf16), "seq", scatter_dimension=2, tiled=True)
    grad_qkv_rows = jnp.concatenate(
        [grad_query.reshape(query.shape)[None].astype(bf16), kv_total.astype(bf16)], axis=0
    )
    grad_qkv = jnp.einsum("srd,csre->cde", u_rows, grad_qkv_rows, preferred_element_type=f32)
    grad_u_part = jnp.einsum("csre,cde->srd", grad_qkv_rows, qkv_w, preferred_element_type=f32)
    part_gain_a = jnp.sum(grad_u_part * (x_wide * scale_a), axis=(0, 1))
    grad_u_all, grad_gain_a, grad_gain_m, grad_router = (
        lax.psum_scatter(
            grad_u_part.astype(jnp.bfloat16), "wa", scatter_dimension=0, tiled=True
        ).astype(jnp.float32),
        lax.psum_scatter(
            part_gain_a.astype(jnp.bfloat16), "wa", scatter_dimension=0, tiled=True
        ).astype(jnp.float32),
        lax.psum_scatter(
            grad_gain_m.astype(jnp.bfloat16), "wa", scatter_dimension=0, tiled=True
        ).astype(jnp.float32),
        lax.psum_scatter(
            grad_router.astype(jnp.bfloat16), "wa", scatter_dimension=0, tiled=True
        ).astype(jnp.float32),
    )
    grad_u_own = grad_u_all[0]
    grad_x_norm, unused = norm_back(x_keep, scale_a[side], gains_a, grad_u_own)
    grad_rows = grad_x_norm + grad_resid + grad_logit[:, None] * w_router.astype(f32)[None, :]
    grad_tokens = cotangent.astype(f32).at[0, own_rows].add(grad_rows).astype(bf16)
    shares = (grad_qkv, grad_out, grad_up, grad_down, grad_gain_a, grad_gain_m, grad_router)
    large = lax.psum(tuple((share.astype(bf16) for share in shares[:4])), "seq")
    small = lax.psum(shares[4:], "seq")
    summed = tuple((part.astype(f32) for part in large)) + small
    return (
        mixed_out,
        grad_tokens,
        summed[0],
        summed[1],
        summed[2],
        summed[3],
        summed[4],
        summed[5],
        summed[6],
    )


def solution(mesh):
    return jax.shard_map(
        body,
        mesh=mesh,
        in_specs=(
            P("wa", "seq", None),
            P("wa", "seq", None),
            P(None, None, "wa"),
            P("wa", None),
            P(None, "wa"),
            P("wa", None),
            P("wa"),
            P("wa"),
            P("wa"),
            P(),
            P(),
        ),
        out_specs=(
            P("wa", "seq", None),
            P("wa", "seq", None),
            P(None, None, "wa"),
            P("wa", None),
            P(None, "wa"),
            P("wa", None),
            P("wa"),
            P("wa"),
            P("wa"),
        ),
        check_vma=False,
    )
```

profile of v0, /device:TPU:0, one launch (start us, length us, event | category | flops | bytes accessed | tf_op | source)
XLA Modules:
  0.0 643.2 jit_solution(9726516830229339342)
XLA Ops:
  21.3 3.2 gather_fusion.2
  27.7 68.0 %all-gather.9.cloned.1.call-done = bf16[2,2,1280,384]{3,2,0,1:T(8,128)(2,1)} async-done(((bf16[2,2,80,384]{3,2,0,1:T(8,128)(2,1)}), bf16[2,2,1280,384]{3,2,0,1:T(8,128)(2,1)}) %all-gather.9.cloned.1.call-update) | async-done | bytes 3932176 | tf_op jit(solution)/shard_map/all_gather | solution.py:72
  95.6 6.3 copy.65
  101.9 14.6 %while.60 = (s32[]{:T(128)}, f32[2,6,80,1]{2,1,0,3:T(8,128)S(1)}, f32[2,6,80,1]{2,1,0,3:T(8,128)S(1)}, s32[2,1280]{1,0:T(2,128)S(1)}, s32[2,80]{1,0:T(2,128)S(1)...) while((s32[]{:T(128)}, f32[2,6,80,1]{2,1,0,3:T(8,128)S(1)}, ...), condition=%wide.region_4.6_spmd.clone, body=%wide.region_1.0_spmd.clone.sunk | while | flops 83922328 | bytes 12404690 | solution.py:100
  117.1 23.4 %while.61 = (s32[]{:T(128)}, f32[2,80,6,64]{1,3,2,0:T(8,128)}, bf16[2,2,1280,384]{2,3,1,0:T(8,128)(2,1)}, s32[2,1280]{1,0:T(2,128)S(1)}, s32[2,80]{1,0:T(2,128)S...) while((s32[]{:T(128)}, f32[2,80,6,64]{1,3,2,0:T(8,128)}, ...), condition=%wide.region_6.8_spmd.clone, body=%wide.region_5.7_spmd.clone.sunk | while | flops 160226000 | bytes 14713809 | solution.py:110
  117.1 4.3 fusion.202
  125.6 3.2 fusion.203
  128.8 4.3 fusion.202
  137.3 3.3 fusion.203
  164.3 2.6 fusion.75
  170.6 11.8 %reduce-scatter.10.cloned.1.call-done = f32[1,80,768]{2,1,0:T(8,128)} async-done(((f32[2,80,768]{2,1,0:T(8,128)}), f32[1,80,768]{2,1,0:T(8,128)}) %reduce-scatter.10.cloned.1.call-update) | async-done | bytes 245776 | tf_op jit(solution)/shard_map/reduce_scatter | solution.py:138
  188.3 15.5 %while.62 = (s32[]{:T(128)}, f32[2,6,80,1]{2,0,1,3:T(2,128)S(1)}, bf16[2,2,1280,384]{2,3,1,0:T(8,128)(2,1)}, bf16[2,80,6,64]{1,3,2,0:T(8,128)(2,1)S(1)}, s32[2,1...) while((s32[]{:T(128)}, f32[2,6,80,1]{2,0,1,3:T(2,128)S(1)}, ...), condition=%wide.region_15.17_spmd.clone, body=%wide.region_13.16_spmd.clone.sunk | while | flops 160718496 | bytes 19275736 | solution.py:155
  188.3 3.7 fusion.208
  196.0 3.7 fusion.208
  206.0 34.5 %while.63 = (s32[]{:T(128)}, f32[2,80,6,64]{1,3,2,0:T(8,128)S(1)}, bf16[2,2,1280,384]{3,2,0,1:T(8,128)(2,1)}, bf16[2,2,1280,384]{2,3,1,0:T(8,128)(2,1)}, s32[2,1...) while((s32[]{:T(128)}, f32[2,80,6,64]{1,3,2,0:T(8,128)S(1)}, ...), condition=%wide.region_17.19_spmd.clone, body=%wide.region_16.18_spmd.clone.sunk | while | flops 401869536 | bytes 60658212 | solution.py:179
  206.0 4.3 fusion.221
  218.9 2.8 copy.95
  223.3 4.3 fusion.221
  236.2 2.8 copy.95
  248.2 128.4 %reduce-scatter.12.cloned.1.call-done = bf16[2,2,80,384]{3,2,0,1:T(8,128)(2,1)} async-done(((bf16[2,2,1280,384]{3,2,0,1:T(8,128)(2,1)}), bf16[2,2,80,384]{3,2,0,1:T(8,128)(2,1)}) %reduce-scatter.12.cloned.1.call-update) | async-done | bytes 245776 | tf_op jit(solution)/shard_map/reduce_scatter | solution.py:185
  390.0 43.3 %all-reduce.4 = (f32[384]{0:T(512)}, f32[384]{0:T(512)}, f32[384]{0:T(512)}) all-reduce(f32[384]{0:T(512)S(1)} %dynamic-slice_convert_fusion.2, f32[384]{0:T(512)S(1)} %get-tuple-element.1100, f32[384]{0:T(512)S(1)} %get-tuple-element.1099), channel_id=1, replica_groups=mesh['seq'=16,'wa'=2] {'seq'}, use_global_device_ids=true, to_apply=%region_29.31 | all-reduce | flops 1152 | bytes 9216 | tf_op jit(solution)/shard_map/psum | solution.py:212
  437.4 186.6 %all-reduce.9.cloned.1.call-done = (bf16[3,768,384]{1,2,0:T(8,128)(2,1)}, bf16[384,768]{1,0:T(8,128)(2,1)}, bf16[768,1536]{1,0:T(8,128)(2,1)}, bf16[1536,768]{1,0:T(8,128)(2,1)}) async-done(((bf16[3,768,384]{1,2,0:T(8,128)(2,1)}, bf16[384,768]{1,0:T(8,128)(2,1)}, bf16[768,1536]{1,0:T(8,128)(2,1)}, bf16[1536,768]{1,0:T(8,128)(2,1)}), (bf16[3,768,384]{1,2,0:T(8,128)(2,1)}, bf16[384,768]{1,0:T(8,128)(2,1)}, ...) | async-done | bytes 7077904 | tf_op jit(solution)/shard_map/psum | solution.py:211
  624.0 4.1 copy.77
  629.2 4.6 convert_element_type.183
  (327 shorter events, 131.5 us)
Async XLA Ops:
  7.2 155.6 %copy-start = (bf16[1536,768]{1,0:T(8,128)(2,1)S(1)}, bf16[1536,768]{1,0:T(8,128)(2,1)}, u32[]{:S(2)}) copy-start(bf16[1536,768]{1,0:T(8,128)(2,1)} %param.26) | copy-start | bytes 7077892
  7.2 88.4 %all-gather.9.cloned.1.call-start = ((), (), s32[]{:S(2)}) async-start(), calls=%async_computation.5 | async-start | bytes 4177920 | tf_op jit(solution)/shard_map/all_gather | solution.py:72
  10.0 16.5 %copy-start.4 = (bf16[80,768]{1,0:T(8,128)(2,1)}, bf16[80,768]{1,0:T(8,128)(2,1)S(1)}, u32[]{:S(2)}) copy-start(bf16[80,768]{1,0:T(8,128)(2,1)S(1)} %gather_fusion.3) | copy-start | bytes 368644
  18.9 136.3 %reduce-scatter.6.cloned.1.call-start = ((), (), s32[]{:S(2)}) async-start(), calls=%async_computation.6 | async-start | bytes 737280 | tf_op jit(solution)/shard_map/reduce_scatter | solution.py:113
  144.5 26.0 %reduce-scatter.8.cloned.1.call-start = ((), (), s32[]{:S(2)}) async-start(), calls=%async_computation.7 | async-start | bytes 368640 | tf_op jit(solution)/shard_map/reduce_scatter | solution.py:121
  156.5 27.8 %copy-start.50 = (f32[80]{0:T(128)}, f32[80]{0:T(128)S(1)}, u32[]{:S(2)}) copy-start(f32[80]{0:T(128)S(1)} %add_rsqrt_fusion.1) | copy-start | bytes 964
  164.2 18.1 %reduce-scatter.10.cloned.1.call-start = ((), (), s32[]{:S(2)}) async-start(), calls=%async_computation.8 | async-start | bytes 737280 | tf_op jit(solution)/shard_map/reduce_scatter | solution.py:138
  167.0 15.4 %copy-start.7 = (f32[1,80,768]{2,1,0:T(8,128)S(1)}, f32[1,80,768]{2,1,0:T(8,128)}, u32[]{:S(2)}) copy-start(f32[1,80,768]{2,1,0:T(8,128)} %reduce-scatter.6.cloned.1.call-done) | copy-start | bytes 737284
  167.0 17.3 %copy-start.54 = (f32[80]{0:T(128)S(1)}, f32[80]{0:T(128)}, u32[]{:S(2)}) copy-start(f32[80]{0:T(128)} %copy-done.53) | copy-start | bytes 964
  167.0 20.6 %copy-start.14 = (bf16[384,768]{1,0:T(8,128)(2,1)S(1)}, bf16[384,768]{1,0:T(8,128)(2,1)}, u32[]{:S(2)}) copy-start(bf16[384,768]{1,0:T(8,128)(2,1)} %param.24) | copy-start | bytes 1769476
  168.7 19.4 %copy-start.38 = (f32[2,6,80,1]{2,1,0,3:T(8,128)S(1)}, f32[2,6,80,1]{2,1,0,3:T(8,128)}, u32[]{:S(2)}) copy-start(f32[2,6,80,1]{2,1,0,3:T(8,128)} %get-tuple-element.1591) | copy-start | bytes 11524
  168.7 207.9 %reduce-scatter.12.cloned.1.call-start = ((), (), s32[]{:S(2)}) async-start(), calls=%async_computation.9 | async-start | bytes 4177920 | tf_op jit(solution)/shard_map/reduce_scatter | solution.py:185
  240.6 192.7 %reduce-scatter.14.cloned.1.call-start = ((), (), s32[]{:S(2)}) async-start(), calls=%async_computation.10 | async-start | bytes 368640 | tf_op jit(solution)/shard_map/reduce_scatter | solution.py:193
  243.9 132.7 %copy-start.21 = (bf16[160,768]{1,0:T(8,128)(2,1)S(1)}, bf16[160,768]{1,0:T(8,128)(2,1)}, u32[]{:S(2)}) copy-start(bf16[160,768]{1,0:T(8,128)(2,1)} %copy-done.20) | copy-start | bytes 737284
  243.9 132.7 %copy-start.26 = (bf16[3,768,384]{2,1,0:T(8,128)(2,1)S(1)}, bf16[3,768,384]{2,1,0:T(8,128)(2,1)}, u32[]{:S(2)}) copy-start(bf16[3,768,384]{2,1,0:T(8,128)(2,1)} %param.23) | copy-start | bytes 5308420
  243.9 132.7 %copy-start.49 = (f32[2,80]{1,0:T(2,128)S(1)}, f32[2,80]{1,0:T(2,128)}, u32[]{:S(2)}) copy-start(f32[2,80]{1,0:T(2,128)} %copy-done.48) | copy-start | bytes 1924
  246.4 132.7 %copy-start.19 = (bf16[160,768]{1,0:T(8,128)(2,1)S(1)}, bf16[160,768]{1,0:T(8,128)(2,1)}, u32[]{:S(2)}) copy-start(bf16[160,768]{1,0:T(8,128)(2,1)} %copy-done.18) | copy-start | bytes 737284
  246.4 132.7 %copy-start.28 = (bf16[2,80,6,64]{1,3,2,0:T(8,128)(2,1)S(1)}, bf16[2,80,6,64]{1,3,2,0:T(8,128)(2,1)}, u32[]{:S(2)}) copy-start(bf16[2,80,6,64]{1,3,2,0:T(8,128)(2,1)} %copy-done.27) | copy-start | bytes 368644
  246.4 133.9 %copy-start.41 = (f32[768]{0:T(1024)S(1)}, f32[768]{0:T(1024)}, u32[]{:S(2)}) copy-start(f32[768]{0:T(1024)} %copy-done.40) | copy-start | bytes 9220
  379.0 245.0 %all-reduce.9.cloned.1.call-start = ((), (), s32[]{:S(2)}) async-start(), calls=%async_computation.11 | async-start | bytes 14155776 | tf_op jit(solution)/shard_map/psum | solution.py:211
  382.3 52.1 %copy-start.17 = (f32[1,80,768]{2,1,0:T(8,128)S(1)}, f32[1,80,768]{2,1,0:T(8,128)}, u32[]{:S(2)}) copy-start(f32[1,80,768]{2,1,0:T(8,128)} %reduce-scatter.10.cloned.1.call-done) | copy-start | bytes 737284
  382.3 52.1 %copy-start.51 = (f32[80]{0:T(128)S(1)}, f32[80]{0:T(128)}, u32[]{:S(2)}) copy-start(f32[80]{0:T(128)} %copy-done.50) | copy-start | bytes 964
  382.3 52.1 %copy-start.57 = (f32[80]{0:T(128)S(1)}, f32[80]{0:T(128)}, u32[]{:S(2)}) copy-start(f32[80]{0:T(128)} %copy-done.56) | copy-start | bytes 964
  386.4 241.7 %copy-start.12 = (bf16[320,768]{1,0:T(8,128)(2,1)}, bf16[320,768]{1,0:T(8,128)(2,1)S(1)}, u32[]{:S(2)}) copy-start(bf16[320,768]{1,0:T(8,128)(2,1)S(1)} %scatter_custom_fusion) | copy-start | bytes 1474564
  (48 other events, 233.7 us)
Sparse Core Ops, SparseCore 0:
  19.1 76.5 all-gather.8
  144.7 6.4 reduce-scatter.5
  164.4 6.1 reduce-scatter.7
  173.3 9.0 reduce-scatter.9
  240.7 135.8 reduce-scatter.11
  379.1 6.7 reduce-scatter.13
  393.0 230.9 all-reduce.8
where the time goes:
time: 645 us; the launch traced here: 643 us
  waiting for transfers between devices  397 us (62%)
  local copies, waits for them, and re-layouts  88.5 us (14%)
  blocking collectives  59.5 us (9%)
  matrix products  44.7 us (7%)
  other arithmetic  37.5 us (6%)
  between operations  15.6 us (2%)
    psum x1, waiting for transfers between devices, body(): large = lax.psum(tuple((share.astype(bf16) for share in shares[:4])), 'seq')  187 us
    reduce_scatter x1, waiting for transfers between devices, body(): lax.psum_scatter(holder.astype(bf16), 'seq', scatter_dimension=2, tiled=T...  128 us
    all_gather x1, waiting for transfers between devices, body(): kv_all = lax.all_gather(local_kv, 'seq', axis=2, tiled=True)  68 us
    psum x1, blocking collectives, body(): small = lax.psum(shares[4:], 'seq')  43.3 us
    unnamed x132, local copies, waits for them, and re-layouts  19.9 us
    slice x6, local copies, waits for them, and re-layouts, block_of(): kv_all[0]  19.3 us
  transfers between devices with their start and end apart: 7, of which 5 were waited for; matrix products, arithmetic and copies ran while one was open for 5% of the time, Pallas kernels for 0%

commit v1 on v0

--- a/solution.py
+++ b/solution.py
@@ -69,7 +69,12 @@
     heads = query.shape[-1] // HD
     factor = HD ** (-0.5)
     split_q = query.reshape(batch, CAP, heads, HD)
-    kv_all = lax.all_gather(local_kv, "seq", axis=2, tiled=True)
+    ring = [local_kv]
+    for hop in range(15):
+        ring.append(lax.ppermute(ring[-1], "seq", [(dev, (dev + 1) % 16) for dev in range(16)]))
+    kv_all = jnp.roll(
+        jnp.concatenate(ring[::-1], axis=2), (lax.axis_index("seq") + 1) * ring[0].shape[2], axis=2
+    )
     block = 8 * CAP
     nblock = kv_all.shape[2] // block
 

time: 645 us -> 731 us (1.13)
  waiting for transfers between devices: 397 us -> 474 us
    ppermute x0 -> x15, waiting for transfers between devices: none -> 149 us  [body(): lax.ppermute(ring[-1], 'seq', [(dev, (dev + 1) % 16) for dev in range(16)])]
    all_gather x1 -> x0, waiting for transfers between devices: 68 us -> none  [body(): kv_all = lax.all_gather(local_kv, 'seq', axis=2, tiled=True)]
    unnamed x132 -> x205, local copies, waits for them, and re-layouts: 19.9 us -> 37.9 us
  transfers between devices with their start and end apart: 7 -> 21, of which waited for: 5 -> 18; matrix products, arithmetic and copies ran while one was open for 5% -> 5% of each run, Pallas kernels for 0% -> 0%
where the time goes in v1:
time: 731 us; the launch traced here: 729 us
  waiting for transfers between devices  474 us (65%)
  local copies, waits for them, and re-layouts  92.5 us (13%)
  blocking collectives  59.6 us (8%)
  matrix products  44.9 us (6%)
  other arithmetic  37.6 us (5%)
  between operations  16 us (2%)
    psum x1, waiting for transfers between devices, body(): large = lax.psum(tuple((share.astype(bf16) for share in shares[:4])), 'seq')  186 us
    ppermute x15, waiting for transfers between devices, body(): lax.ppermute(ring[-1], 'seq', [(dev, (dev + 1) % 16) for dev in range(16)])  149 us
    reduce_scatter x1, waiting for transfers between devices, body(): lax.psum_scatter(holder.astype(bf16), 'seq', scatter_dimension=2, tiled=T...  128 us
    psum x1, blocking collectives, body(): small = lax.psum(shares[4:], 'seq')  43.4 us
    unnamed x205, local copies, waits for them, and re-layouts  37.9 us
  transfers between devices with their start and end apart: 21, of which 18 were waited for; matrix products, arithmetic and copies ran while one was open for 5% of the time, Pallas kernels for 0%

profile of v1, /device:TPU:0, one launch (start us, length us, event | category | flops | bytes accessed | tf_op | source)
XLA Modules:
  0.0 728.7 jit_solution(9952614033133106087)
XLA Ops:
  20.1 10.3 %collective-permute-done = bf16[2,2,80,384]{3,2,0,1:T(8,128)(2,1)S(1)} collective-permute-done((bf16[2,2,80,384]{3,2,0,1:T(8,128)(2,1)S(1)}, bf16[2,2,80,384]{3,2,0,1:T(8,128)(2,1)S(1)}, u32[]{:S(2)}, u32[]{:S(2)}) %collective-permute-start) | collective-permute-done | bytes 245792 | tf_op jit(solution)/shard_map/ppermute | solution.py:74
  31.1 11.1 %collective-permute-done.1 = bf16[2,2,80,384]{3,2,0,1:T(8,128)(2,1)S(1)} collective-permute-done((bf16[2,2,80,384]{3,2,0,1:T(8,128)(2,1)S(1)}, bf16[2,2,80,384]{3,2,0,1:T(8,128)(2,1)S(1)}, u32[]{:S(2)}, u32[]{:S(2)}) %collective-permute-start.1) | collective-permute-done | bytes 245792 | tf_op jit(solution)/shard_map/ppermute | solution.py:74
  42.2 10.3 %collective-permute-done.2 = bf16[2,2,80,384]{3,2,0,1:T(8,128)(2,1)S(1)} collective-permute-done((bf16[2,2,80,384]{3,2,0,1:T(8,128)(2,1)S(1)}, bf16[2,2,80,384]{3,2,0,1:T(8,128)(2,1)S(1)}, u32[]{:S(2)}, u32[]{:S(2)}) %collective-permute-start.2) | collective-permute-done | bytes 245792 | tf_op jit(solution)/shard_map/ppermute | solution.py:74
  52.5 9.8 %collective-permute-done.3 = bf16[2,2,80,384]{3,2,0,1:T(8,128)(2,1)S(1)} collective-permute-done((bf16[2,2,80,384]{3,2,0,1:T(8,128)(2,1)S(1)}, bf16[2,2,80,384]{3,2,0,1:T(8,128)(2,1)S(1)}, u32[]{:S(2)}, u32[]{:S(2)}) %collective-permute-start.3) | collective-permute-done | bytes 245792 | tf_op jit(solution)/shard_map/ppermute | solution.py:74
  63.0 9.8 %collective-permute-done.4 = bf16[2,2,80,384]{3,2,0,1:T(8,128)(2,1)S(1)} collective-permute-done((bf16[2,2,80,384]{3,2,0,1:T(8,128)(2,1)S(1)}, bf16[2,2,80,384]{3,2,0,1:T(8,128)(2,1)S(1)}, u32[]{:S(2)}, u32[]{:S(2)}) %collective-permute-start.4) | collective-permute-done | bytes 245792 | tf_op jit(solution)/shard_map/ppermute | solution.py:74
  73.5 9.8 %collective-permute-done.5 = bf16[2,2,80,384]{3,2,0,1:T(8,128)(2,1)S(1)} collective-permute-done((bf16[2,2,80,384]{3,2,0,1:T(8,128)(2,1)S(1)}, bf16[2,2,80,384]{3,2,0,1:T(8,128)(2,1)S(1)}, u32[]{:S(2)}, u32[]{:S(2)}) %collective-permute-start.5) | collective-permute-done | bytes 245792 | tf_op jit(solution)/shard_map/ppermute | solution.py:74
  84.0 9.8 %collective-permute-done.6 = bf16[2,2,80,384]{3,2,0,1:T(8,128)(2,1)S(1)} collective-permute-done((bf16[2,2,80,384]{3,2,0,1:T(8,128)(2,1)S(1)}, bf16[2,2,80,384]{3,2,0,1:T(8,128)(2,1)S(1)}, u32[]{:S(2)}, u32[]{:S(2)}) %collective-permute-start.6) | collective-permute-done | bytes 245792 | tf_op jit(solution)/shard_map/ppermute | solution.py:74
  94.5 10.7 %collective-permute-done.7 = bf16[2,2,80,384]{3,2,0,1:T(8,128)(2,1)S(1)} collective-permute-done((bf16[2,2,80,384]{3,2,0,1:T(8,128)(2,1)S(1)}, bf16[2,2,80,384]{3,2,0,1:T(8,128)(2,1)S(1)}, u32[]{:S(2)}, u32[]{:S(2)}) %collective-permute-start.7) | collective-permute-done | bytes 245792 | tf_op jit(solution)/shard_map/ppermute | solution.py:74
  105.9 11.9 %collective-permute-done.8 = bf16[2,2,80,384]{3,2,0,1:T(8,128)(2,1)S(1)} collective-permute-done((bf16[2,2,80,384]{3,2,0,1:T(8,128)(2,1)S(1)}, bf16[2,2,80,384]{3,2,0,1:T(8,128)(2,1)S(1)}, u32[]{:S(2)}, u32[]{:S(2)}) %collective-permute-start.8) | collective-permute-done | bytes 245792 | tf_op jit(solution)/shard_map/ppermute | solution.py:74
  118.5 11.8 %collective-permute-done.9 = bf16[2,2,80,384]{3,2,0,1:T(8,128)(2,1)S(1)} collective-permute-done((bf16[2,2,80,384]{3,2,0,1:T(8,128)(2,1)S(1)}, bf16[2,2,80,384]{3,2,0,1:T(8,128)(2,1)S(1)}, u32[]{:S(2)}, u32[]{:S(2)}) %collective-permute-start.9) | collective-permute-done | bytes 245792 | tf_op jit(solution)/shard_map/ppermute | solution.py:74
  131.0 10.6 %collective-permute-done.10 = bf16[2,2,80,384]{3,2,0,1:T(8,128)(2,1)} collective-permute-done((bf16[2,2,80,384]{3,2,0,1:T(8,128)(2,1)S(1)}, bf16[2,2,80,384]{3,2,0,1:T(8,128)(2,1)}, u32[]{:S(2)}, u32[]{:S(2)}) %collective-permute-start.10) | collective-permute-done | bytes 245792 | tf_op jit(solution)/shard_map/ppermute | solution.py:74
  142.3 9.4 %collective-permute-done.11 = bf16[2,2,80,384]{3,2,0,1:T(8,128)(2,1)} collective-permute-done((bf16[2,2,80,384]{3,2,0,1:T(8,128)(2,1)}, bf16[2,2,80,384]{3,2,0,1:T(8,128)(2,1)}, u32[]{:S(2)}, u32[]{:S(2)}) %collective-permute-start.11) | collective-permute-done | bytes 245792 | tf_op jit(solution)/shard_map/ppermute | solution.py:74
  155.0 6.8 collective-permute-done.12
  164.3 7.6 %collective-permute-done.13 = bf16[2,2,80,384]{3,2,0,1:T(8,128)(2,1)} collective-permute-done((bf16[2,2,80,384]{3,2,0,1:T(8,128)(2,1)}, bf16[2,2,80,384]{3,2,0,1:T(8,128)(2,1)}, u32[]{:S(2)}, u32[]{:S(2)}) %collective-permute-start.13) | collective-permute-done | bytes 245792 | tf_op jit(solution)/shard_map/ppermute | solution.py:74
  173.1 8.9 %collective-permute-done.14 = bf16[2,2,80,384]{3,2,0,1:T(8,128)(2,1)} collective-permute-done((bf16[2,2,80,384]{3,2,0,1:T(8,128)(2,1)}, bf16[2,2,80,384]{3,2,0,1:T(8,128)(2,1)}, u32[]{:S(2)}, u32[]{:S(2)}) %collective-permute-start.14) | collective-permute-done | bytes 245792 | tf_op jit(solution)/shard_map/ppermute | solution.py:74
  199.2 6.3 copy.65
  205.5 14.6 %while.60 = (s32[]{:T(128)}, f32[2,6,80,1]{2,1,0,3:T(8,128)S(1)}, f32[2,6,80,1]{2,1,0,3:T(8,128)S(1)}, s32[2,1280]{1,0:T(2,128)S(1)}, s32[2,80]{1,0:T(2,128)S(1)...) while((s32[]{:T(128)}, f32[2,6,80,1]{2,1,0,3:T(8,128)S(1)}, ...), condition=%wide.region_4.6_spmd.clone, body=%wide.region_1.0_spmd.clone.sunk | while | flops 83922328 | bytes 12404682 | solution.py:105
  220.7 16.6 %while.61 = (s32[]{:T(128)}, f32[2,80,6,64]{1,3,2,0:T(8,128)}, bf16[2,2,1280,384]{2,3,1,0:T(8,128)(2,1)}, s32[2,1280]{1,0:T(2,128)S(1)}, s32[2,80]{1,0:T(2,128)S...) while((s32[]{:T(128)}, f32[2,80,6,64]{1,3,2,0:T(8,128)}, ...), condition=%wide.region_6.8_spmd.clone, body=%wide.region_5.7_spmd.clone.sunk | while | flops 160226000 | bytes 14713801 | solution.py:115
  265.8 11.1 %reduce-scatter.10.cloned.1.call-done = f32[1,80,768]{2,1,0:T(8,128)} async-done(((f32[2,80,768]{2,1,0:T(8,128)}), f32[1,80,768]{2,1,0:T(8,128)}) %reduce-scatter.10.cloned.1.call-update) | async-done | bytes 245776 | tf_op jit(solution)/shard_map/reduce_scatter | solution.py:143
  282.6 10.5 %while.62 = (s32[]{:T(128)}, f32[2,6,80,1]{2,0,1,3:T(2,128)S(1)}, bf16[2,2,1280,384]{2,3,1,0:T(8,128)(2,1)}, bf16[2,80,6,64]{1,3,2,0:T(8,128)(2,1)S(1)}, s32[2,1...) while((s32[]{:T(128)}, f32[2,6,80,1]{2,0,1,3:T(2,128)S(1)}, ...), condition=%wide.region_15.17_spmd.clone, body=%wide.region_13.16_spmd.clone.sunk | while | flops 160718496 | bytes 19275728 | solution.py:160
  295.4 30.9 %while.63 = (s32[]{:T(128)}, f32[2,80,6,64]{1,3,2,0:T(8,128)S(1)}, bf16[2,2,1280,384]{3,2,0,1:T(8,128)(2,1)}, bf16[2,2,1280,384]{2,3,1,0:T(8,128)(2,1)}, s32[2,1...) while((s32[]{:T(128)}, f32[2,80,6,64]{1,3,2,0:T(8,128)S(1)}, ...), condition=%wide.region_17.19_spmd.clone, body=%wide.region_16.18_spmd.clone.sunk | while | flops 401869536 | bytes 40997348 | solution.py:184
  333.9 128.3 %reduce-scatter.12.cloned.1.call-done = bf16[2,2,80,384]{3,2,0,1:T(8,128)(2,1)} async-done(((bf16[2,2,1280,384]{3,2,0,1:T(8,128)(2,1)}), bf16[2,2,80,384]{3,2,0,1:T(8,128)(2,1)}) %reduce-scatter.12.cloned.1.call-update) | async-done | bytes 245776 | tf_op jit(solution)/shard_map/reduce_scatter | solution.py:190
  475.6 43.4 %all-reduce.4 = (f32[384]{0:T(512)}, f32[384]{0:T(512)}, f32[384]{0:T(512)}) all-reduce(f32[384]{0:T(512)S(1)} %dynamic-slice_convert_fusion.2, f32[384]{0:T(512)S(1)} %get-tuple-element.1100, f32[384]{0:T(512)S(1)} %get-tuple-element.1099), channel_id=1, replica_groups=mesh['seq'=16,'wa'=2] {'seq'}, use_global_device_ids=true, to_apply=%region_29.31 | all-reduce | flops 1152 | bytes 9216 | tf_op jit(solution)/shard_map/psum | solution.py:217
  523.1 186.3 %all-reduce.9.cloned.1.call-done = (bf16[3,768,384]{1,2,0:T(8,128)(2,1)}, bf16[384,768]{1,0:T(8,128)(2,1)}, bf16[768,1536]{1,0:T(8,128)(2,1)}, bf16[1536,768]{1,0:T(8,128)(2,1)}) async-done(((bf16[3,768,384]{1,2,0:T(8,128)(2,1)}, bf16[384,768]{1,0:T(8,128)(2,1)}, bf16[768,1536]{1,0:T(8,128)(2,1)}, bf16[1536,768]{1,0:T(8,128)(2,1)}), (bf16[3,768,384]{1,2,0:T(8,128)(2,1)}, bf16[384,768]{1,0:T(8,128)(2,1)}, ...) | async-done | bytes 7077904 | tf_op jit(solution)/shard_map/psum | solution.py:216
  (421 shorter events, 188.4 us)
Async XLA Ops:
  7.2 252.6 %copy-start = (bf16[1536,768]{1,0:T(8,128)(2,1)S(1)}, bf16[1536,768]{1,0:T(8,128)(2,1)}, u32[]{:S(2)}) copy-start(bf16[1536,768]{1,0:T(8,128)(2,1)} %param.26) | copy-start | bytes 7077892
  7.2 245.0 %reduce-scatter.6.cloned.1.call-start = ((), (), s32[]{:S(2)}) async-start(), calls=%async_computation.5 | async-start | bytes 737280 | tf_op jit(solution)/shard_map/reduce_scatter | solution.py:118
  10.0 162.0 %copy-start.2 = (bf16[80,768]{1,0:T(8,128)(2,1)}, bf16[80,768]{1,0:T(8,128)(2,1)S(1)}, u32[]{:S(2)}) copy-start(bf16[80,768]{1,0:T(8,128)(2,1)S(1)} %gather_fusion.3) | copy-start | bytes 368644
  17.2 13.2 %collective-permute-start = (bf16[2,2,80,384]{3,2,0,1:T(8,128)(2,1)S(1)}, bf16[2,2,80,384]{3,2,0,1:T(8,128)(2,1)S(1)}, u32[]{:S(2)}, u32[]{:S(2)}) collective-permute-start(bf16[2,2,80,384]{3,2,0,1:T(8,128)(2,1)S(1)} %slice.78), channel_id=1, source_target_pairs={{0,2},{2,4},{4,6},{6,8},{8,10},{10,12},{12,14},{14,16},{16,18},{18... | collective-permute-start | bytes 737288 | tf_op jit(solution)/shard_map/ppermute | solution.py:74
  31.1 11.1 %collective-permute-start.1 = (bf16[2,2,80,384]{3,2,0,1:T(8,128)(2,1)S(1)}, bf16[2,2,80,384]{3,2,0,1:T(8,128)(2,1)S(1)}, u32[]{:S(2)}, u32[]{:S(2)}) collective-permute-start(bf16[2,2,80,384]{3,2,0,1:T(8,128)(2,1)S(1)} %collective-permute-done), channel_id=1, source_target_pairs={{0,2},{2,4},{4,6},{6,8},{8,10},{10,12},{12,14},{14,16},{16,18},{18... | collective-permute-start | bytes 737288 | tf_op jit(solution)/shard_map/ppermute | solution.py:74
  42.2 10.3 %collective-permute-start.2 = (bf16[2,2,80,384]{3,2,0,1:T(8,128)(2,1)S(1)}, bf16[2,2,80,384]{3,2,0,1:T(8,128)(2,1)S(1)}, u32[]{:S(2)}, u32[]{:S(2)}) collective-permute-start(bf16[2,2,80,384]{3,2,0,1:T(8,128)(2,1)S(1)} %collective-permute-done.1), channel_id=1, source_target_pairs={{0,2},{2,4},{4,6},{6,8},{8,10},{10,12},{12,14},{14,16},{16,18},{18... | collective-permute-start | bytes 737288 | tf_op jit(solution)/shard_map/ppermute | solution.py:74
  52.5 9.8 %collective-permute-start.3 = (bf16[2,2,80,384]{3,2,0,1:T(8,128)(2,1)S(1)}, bf16[2,2,80,384]{3,2,0,1:T(8,128)(2,1)S(1)}, u32[]{:S(2)}, u32[]{:S(2)}) collective-permute-start(bf16[2,2,80,384]{3,2,0,1:T(8,128)(2,1)S(1)} %collective-permute-done.2), channel_id=1, source_target_pairs={{0,2},{2,4},{4,6},{6,8},{8,10},{10,12},{12,14},{14,16},{16,18},{18... | collective-permute-start | bytes 737288 | tf_op jit(solution)/shard_map/ppermute | solution.py:74
  63.0 9.8 %collective-permute-start.4 = (bf16[2,2,80,384]{3,2,0,1:T(8,128)(2,1)S(1)}, bf16[2,2,80,384]{3,2,0,1:T(8,128)(2,1)S(1)}, u32[]{:S(2)}, u32[]{:S(2)}) collective-permute-start(bf16[2,2,80,384]{3,2,0,1:T(8,128)(2,1)S(1)} %collective-permute-done.3), channel_id=1, source_target_pairs={{0,2},{2,4},{4,6},{6,8},{8,10},{10,12},{12,14},{14,16},{16,18},{18... | collective-permute-start | bytes 737288 | tf_op jit(solution)/shard_map/ppermute | solution.py:74
  73.5 9.8 %collective-permute-start.5 = (bf16[2,2,80,384]{3,2,0,1:T(8,128)(2,1)S(1)}, bf16[2,2,80,384]{3,2,0,1:T(8,128)(2,1)S(1)}, u32[]{:S(2)}, u32[]{:S(2)}) collective-permute-start(bf16[2,2,80,384]{3,2,0,1:T(8,128)(2,1)S(1)} %collective-permute-done.4), channel_id=1, source_target_pairs={{0,2},{2,4},{4,6},{6,8},{8,10},{10,12},{12,14},{14,16},{16,18},{18... | collective-permute-start | bytes 737288 | tf_op jit(solution)/shard_map/ppermute | solution.py:74
  84.0 9.8 %collective-permute-start.6 = (bf16[2,2,80,384]{3,2,0,1:T(8,128)(2,1)S(1)}, bf16[2,2,80,384]{3,2,0,1:T(8,128)(2,1)S(1)}, u32[]{:S(2)}, u32[]{:S(2)}) collective-permute-start(bf16[2,2,80,384]{3,2,0,1:T(8,128)(2,1)S(1)} %collective-permute-done.5), channel_id=1, source_target_pairs={{0,2},{2,4},{4,6},{6,8},{8,10},{10,12},{12,14},{14,16},{16,18},{18... | collective-permute-start | bytes 737288 | tf_op jit(solution)/shard_map/ppermute | solution.py:74
  94.5 10.7 %collective-permute-start.7 = (bf16[2,2,80,384]{3,2,0,1:T(8,128)(2,1)S(1)}, bf16[2,2,80,384]{3,2,0,1:T(8,128)(2,1)S(1)}, u32[]{:S(2)}, u32[]{:S(2)}) collective-permute-start(bf16[2,2,80,384]{3,2,0,1:T(8,128)(2,1)S(1)} %collective-permute-done.6), channel_id=1, source_target_pairs={{0,2},{2,4},{4,6},{6,8},{8,10},{10,12},{12,14},{14,16},{16,18},{18... | collective-permute-start | bytes 737288 | tf_op jit(solution)/shard_map/ppermute | solution.py:74
  105.9 11.9 %collective-permute-start.8 = (bf16[2,2,80,384]{3,2,0,1:T(8,128)(2,1)S(1)}, bf16[2,2,80,384]{3,2,0,1:T(8,128)(2,1)S(1)}, u32[]{:S(2)}, u32[]{:S(2)}) collective-permute-start(bf16[2,2,80,384]{3,2,0,1:T(8,128)(2,1)S(1)} %collective-permute-done.7), channel_id=1, source_target_pairs={{0,2},{2,4},{4,6},{6,8},{8,10},{10,12},{12,14},{14,16},{16,18},{18... | collective-permute-start | bytes 737288 | tf_op jit(solution)/shard_map/ppermute | solution.py:74
  118.5 11.8 %collective-permute-start.9 = (bf16[2,2,80,384]{3,2,0,1:T(8,128)(2,1)S(1)}, bf16[2,2,80,384]{3,2,0,1:T(8,128)(2,1)S(1)}, u32[]{:S(2)}, u32[]{:S(2)}) collective-permute-start(bf16[2,2,80,384]{3,2,0,1:T(8,128)(2,1)S(1)} %collective-permute-done.8), channel_id=1, source_target_pairs={{0,2},{2,4},{4,6},{6,8},{8,10},{10,12},{12,14},{14,16},{16,18},{18... | collective-permute-start | bytes 737288 | tf_op jit(solution)/shard_map/ppermute | solution.py:74
  131.0 10.6 %collective-permute-start.10 = (bf16[2,2,80,384]{3,2,0,1:T(8,128)(2,1)S(1)}, bf16[2,2,80,384]{3,2,0,1:T(8,128)(2,1)}, u32[]{:S(2)}, u32[]{:S(2)}) collective-permute-start(bf16[2,2,80,384]{3,2,0,1:T(8,128)(2,1)S(1)} %collective-permute-done.9), channel_id=1, source_target_pairs={{0,2},{2,4},{4,6},{6,8},{8,10},{10,12},{12,14},{14,16},{16,18},{18... | collective-permute-start | bytes 737288 | tf_op jit(solution)/shard_map/ppermute | solution.py:74
  141.6 10.1 %collective-permute-start.11 = (bf16[2,2,80,384]{3,2,0,1:T(8,128)(2,1)}, bf16[2,2,80,384]{3,2,0,1:T(8,128)(2,1)}, u32[]{:S(2)}, u32[]{:S(2)}) collective-permute-start(bf16[2,2,80,384]{3,2,0,1:T(8,128)(2,1)} %collective-permute-done.10), channel_id=1, source_target_pairs={{0,2},{2,4},{4,6},{6,8},{8,10},{10,12},{12,14},{14,16},{16,18},{18... | collective-permute-start | bytes 737288 | tf_op jit(solution)/shard_map/ppermute | solution.py:74
  151.7 10.1 %collective-permute-start.12 = (bf16[2,2,80,384]{3,2,0,1:T(8,128)(2,1)}, bf16[2,2,80,384]{3,2,0,1:T(8,128)(2,1)}, u32[]{:S(2)}, u32[]{:S(2)}) collective-permute-start(bf16[2,2,80,384]{3,2,0,1:T(8,128)(2,1)} %collective-permute-done.11), channel_id=1, source_target_pairs={{0,2},{2,4},{4,6},{6,8},{8,10},{10,12},{12,14},{14,16},{16,18},{18... | collective-permute-start | bytes 737288 | tf_op jit(solution)/shard_map/ppermute | solution.py:74
  161.8 10.1 %collective-permute-start.13 = (bf16[2,2,80,384]{3,2,0,1:T(8,128)(2,1)}, bf16[2,2,80,384]{3,2,0,1:T(8,128)(2,1)}, u32[]{:S(2)}, u32[]{:S(2)}) collective-permute-start(bf16[2,2,80,384]{3,2,0,1:T(8,128)(2,1)} %collective-permute-done.12), channel_id=1, source_target_pairs={{0,2},{2,4},{4,6},{6,8},{8,10},{10,12},{12,14},{14,16},{16,18},{18... | collective-permute-start | bytes 737288 | tf_op jit(solution)/shard_map/ppermute | solution.py:74
  171.9 10.1 %collective-permute-start.14 = (bf16[2,2,80,384]{3,2,0,1:T(8,128)(2,1)}, bf16[2,2,80,384]{3,2,0,1:T(8,128)(2,1)}, u32[]{:S(2)}, u32[]{:S(2)}) collective-permute-start(bf16[2,2,80,384]{3,2,0,1:T(8,128)(2,1)} %collective-permute-done.13), channel_id=1, source_target_pairs={{0,2},{2,4},{4,6},{6,8},{8,10},{10,12},{12,14},{14,16},{16,18},{18... | collective-permute-start | bytes 737288 | tf_op jit(solution)/shard_map/ppermute | solution.py:74
  241.3 24.5 %reduce-scatter.8.cloned.1.call-start = ((), (), s32[]{:S(2)}) async-start(), calls=%async_computation.6 | async-start | bytes 368640 | tf_op jit(solution)/shard_map/reduce_scatter | solution.py:126
  261.2 15.7 %reduce-scatter.10.cloned.1.call-start = ((), (), s32[]{:S(2)}) async-start(), calls=%async_computation.7 | async-start | bytes 737280 | tf_op jit(solution)/shard_map/reduce_scatter | solution.py:143
  265.7 196.5 %reduce-scatter.12.cloned.1.call-start = ((), (), s32[]{:S(2)}) async-start(), calls=%async_computation.8 | async-start | bytes 4177920 | tf_op jit(solution)/shard_map/reduce_scatter | solution.py:190
  326.3 192.6 %reduce-scatter.14.cloned.1.call-start = ((), (), s32[]{:S(2)}) async-start(), calls=%async_computation.9 | async-start | bytes 368640 | tf_op jit(solution)/shard_map/reduce_scatter | solution.py:198
  464.6 244.8 %all-reduce.9.cloned.1.call-start = ((), (), s32[]{:S(2)}) async-start(), calls=%async_computation.10 | async-start | bytes 14155776 | tf_op jit(solution)/shard_map/psum | solution.py:216
  472.0 242.1 %copy-start.10 = (bf16[320,768]{1,0:T(8,128)(2,1)}, bf16[320,768]{1,0:T(8,128)(2,1)S(1)}, u32[]{:S(2)}) copy-start(bf16[320,768]{1,0:T(8,128)(2,1)S(1)} %scatter_custom_fusion) | copy-start | bytes 1474564
  (79 other events, 2222.0 us)
Sparse Core Ops, SparseCore 0:
  241.4 3.7 reduce-scatter.5
  261.3 3.5 reduce-scatter.7
  267.8 9.0 reduce-scatter.9
  326.4 135.6 reduce-scatter.11
  464.8 6.7 reduce-scatter.13
  478.4 230.9 all-reduce.8
